TPU v7x, 256 devices: a whole 4x4x8 slice. The times are simulated.
256 devices in a mesh: rows: 64 (over x_hi, y, z), grp: 4 (over x_lo, core).
Axes of the slice: x: 4 (x_hi: 2, x_lo: 2; x = x_hi * 2 + x_lo), y: 4, z: 8, core: 2. Of those that a mesh axis runs over, the one named last changes fastest.
Arguments:
- table: float32 [524288, 256], P(('rows', 'grp')), may hold values from -1.5 to 1.5
- hot_slot: int32 [4096], P(('rows', 'grp')), may hold values from 0 to 2047, as said below
- cold_row: int32 [256, 256, 8], P(('rows', 'grp')), may hold values from 0 to 2047, as said below
- cold_bag: int32 [256, 256, 8], P(('rows', 'grp')), may hold values from 0 to 511
- hot_pick: int32 [65536, 8], P(('rows', 'grp')), may hold values from 0 to 4095
- dense: float32 [65536, 256], P(('rows', 'grp')), may hold values from -6 to 6
- label: int32 [65536], P(('rows', 'grp')), may hold values 0 or 1
Outputs:
- pooled: float32 [65536, 256], P(('rows', 'grp'))
- new_table: float32 [524288, 256], P(('rows', 'grp'))
- hot_new: float32 [4096, 256], replicated
Inputs may be any that keep to these rules, and one draw needn't show every extreme that they name: `hot_slot`: distinct within each device's block of 16 entries; hot row h lies in the shard of device h // 16. `cold_row`: a cold slot never names a hot row of its owner. `cold_bag`: a value of 256 or more marks an empty slot.
All inputs are finite; a program needn't handle non-finite values. No bound on the sum of `label` on one device may be relied on, other than what follows from the above.
Results may differ from a plain program's by a relative error of at most 0.0029.
Values may be sent and summed in bfloat16 or wider, within the bound.
A program may use at most 64 MiB of HBM per device.

v0:
```python
import jax
import jax.numpy as jnp
from jax import lax
from jax.sharding import PartitionSpec as P


def split_up(value, dim, peers):
    shape = value.shape
    blocks = value.reshape(*shape[:dim], peers, shape[dim] // peers, *shape[dim + 1 :])
    return jnp.moveaxis(blocks, dim, 0)


def laid_out(blocks, dim):
    blocks = jnp.moveaxis(blocks, 0, dim)
    shape = blocks.shape
    return blocks.reshape(*shape[:dim], shape[dim] * shape[dim + 1], *shape[dim + 2 :])


def exchange_both(value, axis, axes, splits, concats):
    sizes = [lax.axis_size(a) for a in axes]
    blocks = split_up(value, splits[0], sizes[0])
    blocks = jnp.moveaxis(split_up(blocks, splits[1] + 1, sizes[1]), 0, 1)
    inside = blocks.shape[2:]
    blocks = blocks.reshape(-1, *inside)
    blocks = lax.all_to_all(blocks, axis, split_axis=0, concat_axis=0, tiled=True)
    blocks = laid_out(blocks.reshape(*sizes, *inside), concats[0] + 1)
    return laid_out(blocks, concats[1])


def body(table, hot_slot, cold_row, cold_bag, hot_pick, dense, label):
    n_rows = lax.axis_size("rows")
    n_grp = lax.axis_size("grp")
    width = table.shape[1]
    samples = dense.shape[0]
    own_hot = hot_slot.shape[0]
    slots = cold_row.shape[1] * cold_row.shape[2]
    per_peer = cold_row.shape[2]
    rounded = table.astype(jnp.bfloat16)
    hot_full = lax.all_gather(table[hot_slot], ("rows", "grp"), axis=0, tiled=True)
    hot_copy = hot_full.astype(jnp.bfloat16)
    requests = cold_row[0].reshape(n_rows, n_grp, per_peer)
    arrived = exchange_both(requests, ("rows", "grp"), ("rows", "grp"), (0, 1), (0, 1))
    looked = rounded[arrived.reshape(-1)].reshape(n_rows, n_grp, per_peer, width)
    returned = lax.all_to_all(
        lax.all_to_all(looked, "rows", split_axis=0, concat_axis=0, tiled=True),
        "grp",
        split_axis=1,
        concat_axis=1,
        tiled=True,
    )
    flat_rows = returned.reshape(slots, width)
    bags = cold_bag[0].reshape(slots)
    selector = jnp.arange(samples, dtype=jnp.int32)[:, None] == bags[None, :]
    cold_pooled = jnp.dot(
        selector.astype(jnp.bfloat16), flat_rows, preferred_element_type=jnp.float32
    )
    hot_pooled = jnp.sum(hot_copy[hot_pick].astype(jnp.float32), axis=1)
    pooled = cold_pooled + hot_pooled
    score = jnp.sum(pooled * dense, axis=1) / width**0.5
    err = jax.nn.sigmoid(score) - label.astype(jnp.float32)
    grad = err[:, None] * dense
    slot_grad = lax.dot_general(
        selector.astype(jnp.float32),
        grad,
        (((0,), (0,)), ((), ())),
        precision=lax.Precision.HIGHEST,
        preferred_element_type=jnp.float32,
    )
    delivered = exchange_both(
        slot_grad.reshape(n_rows, n_grp, per_peer, width),
        ("rows", "grp"),
        ("rows", "grp"),
        (0, 1),
        (0, 1),
    )
    table_grad = jax.ops.segment_sum(
        delivered.reshape(slots, width), arrived.reshape(slots), num_segments=table.shape[0]
    )
    hot_total = hot_copy.shape[0]
    spread = jnp.repeat(grad, hot_pick.shape[1], axis=0)
    hot_local = jax.ops.segment_sum(spread, hot_pick.reshape(-1), num_segments=hot_total)
    summed = lax.psum(hot_local, ("rows", "grp"))
    start = lax.axis_index(("rows", "grp")) * own_hot
    own_grad = lax.dynamic_slice_in_dim(summed, start, own_hot, 0)
    table_grad = table_grad.at[hot_slot].add(own_grad)
    new_table = table - 0.1 * table_grad
    hot_new = hot_full - 0.1 * summed
    return (pooled, new_table, hot_new)


def solution(mesh):
    placed = (
        P(("rows", "grp"), None),
        P(("rows", "grp")),
        P(("rows", "grp"), None, None),
        P(("rows", "grp"), None, None),
        P(("rows", "grp"), None),
        P(("rows", "grp"), None),
        P(("rows", "grp")),
    )
    return jax.shard_map(
        body,
        mesh=mesh,
        in_specs=placed,
        out_specs=(P(("rows", "grp"), None), P(("rows", "grp"), None), P()),
        check_vma=False,
    )
```

profile of v0, /device:TPU:2, one launch (start us, length us, event | category | flops | bytes accessed | tf_op | source)
XLA Modules:
  0.0 783.1 jit_solution(3402326476514333365)
XLA Ops:
  8.4 2.8 gather_fusion.1
  11.2 1.5 copy.38
  12.7 14.7 %all-to-all-start = ((s32[256,1,1,8]{3,2,1,0:T(1,128)}), s32[256,1,1,8]{3,2,1,0:T(1,128)S(1)}, u32[]{:S(2)}, u32[]{:S(2)}) async-start(s32[256,1,1,8]{3,2,1,0:T(1,128)} %bitcast), calls=%async_computation | async-start | bytes 262144 | tf_op jit(solution)/shard_map/all_to_all | solution.py:25
  27.4 1.7 convert_element_type.14
  29.1 10.6 %all-to-all-done = s32[256,1,1,8]{3,2,1,0:T(1,128)S(1)} async-done(((s32[256,1,1,8]{3,2,1,0:T(1,128)}), s32[256,1,1,8]{3,2,1,0:T(1,128)S(1)}, u32[]{:S(2)}, u32[]{:S(2)}) %all-to-all-start) | async-done | bytes 8224 | tf_op jit(solution)/shard_map/all_to_all | solution.py:25
  39.8 7.5 gather_fusion
  47.3 34.3 %all_to_all.20 = bf16[64,4,8,256]{3,2,1,0:T(8,128)(2,1)S(1)} all-to-all(bf16[64,4,8,256]{3,2,1,0:T(8,128)(2,1)S(1)} %bitcast.38), channel_id=1, replica_groups=mesh['rows'=64,'grp'=4] {'rows'}, dimensions={0} | all-to-all | bytes 2097152 | tf_op jit(solution)/shard_map/all_to_all | solution.py:45
  81.6 1.0 copy.39
  82.6 4.7 all-to-all-start.2
  88.7 12.2 %all-to-all-done.2 = bf16[64,4,8,256]{3,2,0,1:T(8,128)(2,1)S(1)} async-done(((bf16[64,4,8,256]{3,2,0,1:T(8,128)(2,1)}), bf16[64,4,8,256]{3,2,0,1:T(8,128)(2,1)S(1)}, u32[]{:S(2)}, u32[]{:S(2)}) %all-to-all-start.2) | async-done | bytes 1048608 | tf_op jit(solution)/shard_map/all_to_all | solution.py:44
  100.9 1.1 copy.40
  102.0 330.1 %all-gather.3.cloned.1.call-done = f32[4096,256]{1,0:T(8,128)} async-done(((f32[16,256]{1,0:T(8,128)}), f32[4096,256]{1,0:T(8,128)}) %all-gather.3.cloned.1.call-update) | async-done | bytes 4194320 | tf_op jit(solution)/shard_map/all_gather | solution.py:39
  432.1 2.4 convert_element_type.15
  434.5 7.5 gather_fusion.2
  442.9 2.0 multiply_reduce_fusion
  445.0 3.2 fusion.7
  448.2 9.4 %all-to-all-start.3 = ((f32[256,1,1,8,256]{4,3,2,1,0:T(8,128)}), f32[256,1,1,8,256]{4,3,2,1,0:T(8,128)S(1)}, u32[]{:S(2)}, u32[]{:S(2)}) async-start(f32[256,1,1,8,256]{4,3,2,1,0:T(8,128)} %fusion.7), calls=%async_computation.3 | async-start | bytes 4194304 | tf_op jit(solution)/shard_map/all_to_all | solution.py:25
  458.0 13.8 %scatter_custom_fusion.1 = f32[4096,256]{1,0:T(8,128)} fusion(s32[2048]{0:T(1024)S(1)} %reshape.98, f32[]{:T(128)} %constant.15.clone.1, f32[256,256]{1,0:T(8,128)S(1)} %broadcast_multiply_fusion), kind=kCustom, calls=%fused_computation.10 | custom fusion | flops 524288 | bytes 4456452 | tf_op jit(solution)/shard_map/scatter-add | solution.py:81
  472.0 0.8 copy.46
  472.9 277.2 %all-reduce.2.cloned.1.call-done = f32[4096,256]{1,0:T(8,128)} async-done(((f32[4096,256]{1,0:T(8,128)}), f32[4096,256]{1,0:T(8,128)}) %all-reduce.2.cloned.1.call-update) | async-done | bytes 4194320 | tf_op jit(solution)/shard_map/psum | solution.py:82
  750.1 6.0 multiply_subtract_fusion
  756.1 13.0 %scatter_custom_fusion = f32[2048,256]{1,0:T(8,128)} fusion(s32[2048]{0:T(1024)S(1)} %reshape.90, f32[256,1,1,8,256]{4,3,2,1,0:T(8,128)S(1)} %all-to-all-done.3, f32[]{:T(128)} %constant.15.clone.1), kind=kCustom, calls=%fused_computation.7 | custom fusion | flops 524288 | bytes 4194308 | tf_op jit(solution)/shard_map/scatter-add | solution.py:76
  769.2 3.9 scatter_custom_fusion.2
  773.0 3.2 multiply_subtract_fusion.1
  (38 shorter events, 4.3 us)
Async XLA Ops:
  7.2 425.0 %all-gather.3.cloned.1.call-start = ((), (), s32[]{:S(2)}) async-start(), calls=%async_computation.5 | async-start | bytes 4210688 | tf_op jit(solution)/shard_map/all_gather | solution.py:39
  7.9 0.5 copy-start.6
  12.7 27.0 %all-to-all-start = ((s32[256,1,1,8]{3,2,1,0:T(1,128)}), s32[256,1,1,8]{3,2,1,0:T(1,128)S(1)}, u32[]{:S(2)}, u32[]{:S(2)}) async-start(s32[256,1,1,8]{3,2,1,0:T(1,128)} %bitcast), calls=%async_computation | async-start | bytes 262144 | tf_op jit(solution)/shard_map/all_to_all | solution.py:25
  81.6 5.7 copy-start.1
  81.6 6.6 copy-start.2
  81.6 6.8 copy-start.4
  82.6 18.3 %all-to-all-start.2 = ((bf16[64,4,8,256]{3,2,0,1:T(8,128)(2,1)}), bf16[64,4,8,256]{3,2,0,1:T(8,128)(2,1)S(1)}, u32[]{:S(2)}, u32[]{:S(2)}) async-start(bf16[64,4,8,256]{3,2,0,1:T(8,128)(2,1)} %copy.39), calls=%async_computation.2 | async-start | bytes 2097152 | tf_op jit(solution)/shard_map/all_to_all | solution.py:44
  442.0 2.8 copy-start.5
  448.2 9.6 %copy-start.3 = (s32[256,8]{0,1:T(8,128)S(1)}, s32[256,8]{0,1:T(8,128)}, u32[]{:S(2)}) copy-start(s32[256,8]{0,1:T(8,128)} %param.11) | copy-start | bytes 24580
  448.2 308.0 %all-to-all-start.3 = ((f32[256,1,1,8,256]{4,3,2,1,0:T(8,128)}), f32[256,1,1,8,256]{4,3,2,1,0:T(8,128)S(1)}, u32[]{:S(2)}, u32[]{:S(2)}) async-start(f32[256,1,1,8,256]{4,3,2,1,0:T(8,128)} %fusion.7), calls=%async_computation.3 | async-start | bytes 4194304 | tf_op jit(solution)/shard_map/all_to_all | solution.py:25
  457.5 292.6 %all-reduce.2.cloned.1.call-start = ((), (), s32[]{:S(2)}) async-start(), calls=%async_computation.4 | async-start | bytes 8388608 | tf_op jit(solution)/shard_map/psum | solution.py:82
  769.2 3.9 copy-start
Sparse Core Ops, SparseCore 0:
  11.3 420.7 all-gather.2
  472.0 278.0 all-reduce.1
where the time goes:
time: 784 us; the launch traced here: 783 us
  waiting for transfers between devices  630 us (80%)
  other arithmetic  45.5 us (6%)
  blocking collectives  34.3 us (4%)
  starting transfers between devices  29 us (4%)
  local copies, waits for them, and re-layouts  24.8 us (3%)
  between operations  14.2 us (2%)
    all_gather x1, waiting for transfers between devices, body(): lax.all_gather(table[hot_slot], ('rows', 'grp'), axis=0, tiled=True)  330 us
    psum x1, waiting for transfers between devices, body(): summed = lax.psum(hot_local, ('rows', 'grp'))  277 us
    all_to_all x1, blocking collectives, body(): lax.all_to_all(looked, 'rows', split_axis=0, concat_axis=0, tiled=True)  34.3 us
    all_to_all x2, starting transfers between devices, exchange_both(): lax.all_to_all(blocks, axis, split_axis=0, concat_axis=0, tiled=True)  24 us
  transfers between devices with their start and end apart: 5, of which 4 were waited for; matrix products, arithmetic and copies ran while one was open for 5% of the time, Pallas kernels for 0%

commit v1 on v0

--- a/solution.py
+++ b/solution.py
@@ -79,7 +79,7 @@
     hot_total = hot_copy.shape[0]
     spread = jnp.repeat(grad, hot_pick.shape[1], axis=0)
     hot_local = jax.ops.segment_sum(spread, hot_pick.reshape(-1), num_segments=hot_total)
-    summed = lax.psum(hot_local, ("rows", "grp"))
+    summed = lax.psum(lax.psum(hot_local, "grp"), "rows")
     start = lax.axis_index(("rows", "grp")) * own_hot
     own_grad = lax.dynamic_slice_in_dim(summed, start, own_hot, 0)
     table_grad = table_grad.at[hot_slot].add(own_grad)

time: 784 us -> 1290 us (1.65)
  waiting for transfers between devices: 630 us -> 1130 us
    psum x1 -> x2, waiting for transfers between devices: 277 us -> 722 us  [body(): summed = lax.psum(lax.psum(hot_local, 'grp'), 'rows')]
    all_to_all x2, waiting for transfers between devices: 10.6 us -> 69.1 us  [exchange_both(): lax.all_to_all(blocks, axis, split_axis=0, concat_axis=0, tiled=True)]
  transfers between devices with their start and end apart: 5 -> 6, of which waited for: 4 -> 6; matrix products, arithmetic and copies ran while one was open for 5% -> 3% of each run, Pallas kernels for 0% -> 0%
where the time goes in v1:
time: 1290 us
  waiting for transfers between devices  1130 us (88%)
  other arithmetic  44.4 us (3%)
  blocking collectives  34.3 us (3%)
  starting transfers between devices  33.8 us (3%)
  local copies, waits for them, and re-layouts  25.4 us (2%)
  between operations  13.9 us (1%)
    psum x2, waiting for transfers between devices, body(): summed = lax.psum(lax.psum(hot_local, 'grp'), 'rows')  722 us
    all_gather x1, waiting for transfers between devices, body(): lax.all_gather(table[hot_slot], ('rows', 'grp'), axis=0, tiled=True)  330 us
    all_to_all x2, waiting for transfers between devices, exchange_both(): lax.all_to_all(blocks, axis, split_axis=0, concat_axis=0, tiled=True)  69.1 us
    all_to_all x1, blocking collectives, body(): lax.all_to_all(looked, 'rows', split_axis=0, concat_axis=0, tiled=True)  34.3 us
    all_to_all x2, starting transfers between devices, exchange_both(): lax.all_to_all(blocks, axis, split_axis=0, concat_axis=0, tiled=True)  29 us
  transfers between devices with their start and end apart: 6, of which 6 were waited for; matrix products, arithmetic and copies ran while one was open for 3% of the time, Pallas kernels for 0%

profile of v1, /device:TPU:2, one launch (start us, length us, event | category | flops | bytes accessed | tf_op | source)
XLA Modules:
  0.0 1289.9 jit_solution(18073150162778733575)
XLA Ops:
  8.5 2.8 gather_fusion.1
  11.2 1.5 copy.38
  12.7 14.7 %all-to-all-start = ((s32[256,1,1,8]{3,2,1,0:T(1,128)}), s32[256,1,1,8]{3,2,1,0:T(1,128)S(1)}, u32[]{:S(2)}, u32[]{:S(2)}) async-start(s32[256,1,1,8]{3,2,1,0:T(1,128)} %bitcast), calls=%async_computation | async-start | bytes 262144 | tf_op jit(solution)/shard_map/all_to_all | solution.py:25
  27.4 1.7 convert_element_type.14
  29.1 10.6 all-to-all-done
  39.9 7.5 gather_fusion
  47.4 34.3 %all_to_all.20 = bf16[64,4,8,256]{3,2,1,0:T(8,128)(2,1)S(1)} all-to-all(bf16[64,4,8,256]{3,2,1,0:T(8,128)(2,1)S(1)} %bitcast.38), channel_id=1, replica_groups=mesh['rows'=64,'grp'=4] {'rows'}, dimensions={0} | all-to-all | bytes 2097152 | tf_op jit(solution)/shard_map/all_to_all | solution.py:45
  82.7 4.7 all-to-all-start.2
  89.6 11.4 all-to-all-done.2
  101.0 1.1 copy.40
  102.1 330.1 %all-gather.3.cloned.1.call-done = f32[4096,256]{1,0:T(8,128)} async-done(((f32[16,256]{1,0:T(8,128)}), f32[4096,256]{1,0:T(8,128)}) %all-gather.3.cloned.1.call-update) | async-done | bytes 4194320 | tf_op jit(solution)/shard_map/all_gather | solution.py:39
  432.2 2.4 convert_element_type.15
  434.6 7.5 gather_fusion.2
  443.0 2.0 multiply_reduce_fusion
  445.1 14.0 %scatter_custom_fusion.1 = f32[4096,256]{1,0:T(8,128)} fusion(s32[2048]{0:T(1024)} %reshape.98, f32[]{:T(128)} %constant.15.clone.1, f32[256,256]{1,0:T(8,128)S(1)} %broadcast_multiply_fusion), kind=kCustom, calls=%fused_computation.10 | custom fusion | flops 524288 | bytes 4456960 | tf_op jit(solution)/shard_map/scatter-add | solution.py:81
  459.1 92.4 %all-reduce.3.cloned.1.call-done = f32[4096,256]{1,0:T(8,128)} async-done(((f32[4096,256]{1,0:T(8,128)}), f32[4096,256]{1,0:T(8,128)}) %all-reduce.3.cloned.1.call-update) | async-done | bytes 4194320 | tf_op jit(solution)/shard_map/psum | solution.py:82
  551.6 3.2 fusion.7
  554.7 14.3 %all-to-all-start.3 = ((f32[256,1,1,8,256]{4,3,2,1,0:T(8,128)}), f32[256,1,1,8,256]{4,3,2,1,0:T(8,128)S(1)}, u32[]{:S(2)}, u32[]{:S(2)}) async-start(f32[256,1,1,8,256]{4,3,2,1,0:T(8,128)} %fusion.7), calls=%async_computation.3 | async-start | bytes 4194304 | tf_op jit(solution)/shard_map/all_to_all | solution.py:25
  570.0 58.5 %all-to-all-done.3 = f32[256,1,1,8,256]{4,3,2,1,0:T(8,128)S(1)} async-done(((f32[256,1,1,8,256]{4,3,2,1,0:T(8,128)}), f32[256,1,1,8,256]{4,3,2,1,0:T(8,128)S(1)}, u32[]{:S(2)}, u32[]{:S(2)}) %all-to-all-start.3) | async-done | bytes 2097184 | tf_op jit(solution)/shard_map/all_to_all | solution.py:25
  628.5 13.0 %scatter_custom_fusion = f32[2048,256]{1,0:T(8,128)} fusion(s32[2048]{0:T(1024)S(1)} %reshape.90, f32[256,1,1,8,256]{4,3,2,1,0:T(8,128)S(1)} %all-to-all-done.3, f32[]{:T(128)} %constant.15.clone.1), kind=kCustom, calls=%fused_computation.7 | custom fusion | flops 524288 | bytes 4194308 | tf_op jit(solution)/shard_map/scatter-add | solution.py:76
  641.5 630.0 %all-reduce.5.cloned.1.call-done = f32[4096,256]{1,0:T(8,128)} async-done(((f32[4096,256]{1,0:T(8,128)}), f32[4096,256]{1,0:T(8,128)}) %all-reduce.5.cloned.1.call-update) | async-done | bytes 4194320 | tf_op jit(solution)/shard_map/psum | solution.py:82
  1271.5 3.7 scatter_custom_fusion.2
  1275.3 3.3 multiply_subtract_fusion.1
  1278.6 4.7 multiply_subtract_fusion
  (41 shorter events, 6.7 us)
Async XLA Ops:
  7.2 425.1 %all-gather.3.cloned.1.call-start = ((), (), s32[]{:S(2)}) async-start(), calls=%async_computation.6 | async-start | bytes 4210688 | tf_op jit(solution)/shard_map/all_gather | solution.py:39
  7.9 0.6 copy-start.6
  12.7 27.0 %all-to-all-start = ((s32[256,1,1,8]{3,2,1,0:T(1,128)}), s32[256,1,1,8]{3,2,1,0:T(1,128)S(1)}, u32[]{:S(2)}, u32[]{:S(2)}) async-start(s32[256,1,1,8]{3,2,1,0:T(1,128)} %bitcast), calls=%async_computation | async-start | bytes 262144 | tf_op jit(solution)/shard_map/all_to_all | solution.py:25
  81.7 5.8 copy-start.2
  81.7 6.6 copy-start.3
  81.7 7.0 copy-start.4
  82.7 18.3 %all-to-all-start.2 = ((bf16[64,4,8,256]{3,2,0,1:T(8,128)(2,1)}), bf16[64,4,8,256]{3,2,0,1:T(8,128)(2,1)S(1)}, u32[]{:S(2)}, u32[]{:S(2)}) async-start(bf16[64,4,8,256]{3,2,0,1:T(8,128)(2,1)} %copy.39), calls=%async_computation.2 | async-start | bytes 2097152 | tf_op jit(solution)/shard_map/all_to_all | solution.py:44
  87.4 464.1 %all-reduce.3.cloned.1.call-start = ((), (), s32[]{:S(2)}) async-start(), calls=%async_computation.4 | async-start | bytes 8388608 | tf_op jit(solution)/shard_map/psum | solution.py:82
  442.1 2.8 copy-start.5
  459.1 812.4 %all-reduce.5.cloned.1.call-start = ((), (), s32[]{:S(2)}) async-start(), calls=%async_computation.5 | async-start | bytes 8388608 | tf_op jit(solution)/shard_map/psum | solution.py:82
  554.7 73.8 %all-to-all-start.3 = ((f32[256,1,1,8,256]{4,3,2,1,0:T(8,128)}), f32[256,1,1,8,256]{4,3,2,1,0:T(8,128)S(1)}, u32[]{:S(2)}, u32[]{:S(2)}) async-start(f32[256,1,1,8,256]{4,3,2,1,0:T(8,128)} %fusion.7), calls=%async_computation.3 | async-start | bytes 4194304 | tf_op jit(solution)/shard_map/all_to_all | solution.py:25
  641.5 633.7 %copy-start.1 = (f32[2048,256]{1,0:T(8,128)S(1)}, f32[2048,256]{1,0:T(8,128)}, u32[]{:S(2)}) copy-start(f32[2048,256]{1,0:T(8,128)} %param.7) | copy-start | bytes 6291460
  1275.3 3.3 copy-start
Sparse Core Ops, SparseCore 0:
  11.4 420.8 all-gather.2
  459.2 92.2 all-reduce.2
  554.2 717.3 all-reduce.4
